TPU v7x, 32 devices: a whole 2x2x4 slice. The times are simulated.
32 devices in a mesh: dp: 8 (over y, x, core), head: 4 (over z).
Axes of the slice: x: 2, y: 2, z: 4, core: 2. Of those that a mesh axis runs over, the one named last changes fastest.
Arguments:
- tokens_in: bfloat16 [16384, 768], P(('dp', 'head')), may hold values from -6 to 6
- gain_attn: float32 [768], replicated, may hold values from 0.1 to 1.9
- gain_ffn: float32 [768], replicated, may hold values from 0.1 to 1.9
- w_qkv: bfloat16 [3, 768, 768], P(None, None, 'head'), may hold values from -0.3125 to 0.3125
- w_out: bfloat16 [768, 768], P('head'), may hold values from -0.5 to 0.5
- w_up: bfloat16 [768, 768], replicated, may hold values from -0.21875 to 0.21875
- w_down: bfloat16 [768, 768], replicated, may hold values from -0.21875 to 0.21875
- slot_mol: int32 [8, 16], P('dp'), may hold values from 0 to 11, never falling along the last dimension, each value on 1 to 2 neighbouring positions
- slot_fill: int32 [8, 16], P('dp'), may hold values from 16 to 128
- cotangent: bfloat16 [16384, 768], P(('dp', 'head')), may hold values from -6 to 6
Outputs:
- layer_out: bfloat16 [16384, 768], P(('dp', 'head'))
- d_tokens: float32 [16384, 768], P(('dp', 'head'))
- d_gain_attn: float32 [768], replicated
- d_gain_ffn: float32 [768], replicated
- d_w_qkv: float32 [3, 768, 768], P(None, None, 'head')
- d_w_out: float32 [768, 768], P('head')
- d_w_up: float32 [768, 768], replicated
- d_w_down: float32 [768, 768], replicated
Inputs may be any that keep to these rules, and one draw needn't show every extreme that they name: `slot_mol`: each group holds 12 molecules numbered in slot order; a molecule takes one slot or two consecutive slots. `slot_fill`: the live tokens of a slot are its first rows.
All inputs are finite; a program needn't handle non-finite values.
Results may differ from a plain program's by a relative error of at most 0.015.
The roundings to bfloat16 on the way count: a program that leaves them out, or rounds other values in their place, can miss the bound.
Values may be sent and summed in bfloat16 or wider, within the bound.
A program may use at most 128 MiB of HBM per device.

v0:
```python
import jax
import jax.numpy as jnp
from jax import lax
from jax.sharding import PartitionSpec as P

HEAD_DIM = 24
SLOT_LEN = 128
epsilon = 1e-05
masked_score = -1000000000.0


def layer_norm(values, scale_gain):
    row_mean = jnp.mean(values, axis=-1, keepdims=True)
    centred = values - row_mean
    variance = jnp.mean(centred * centred, axis=-1, keepdims=True)
    return centred * lax.rsqrt(variance + epsilon) * scale_gain


def gelu_exact(values):
    return jax.nn.gelu(values, approximate=False)


def local(
    tokens_in, gain_attn, gain_ffn, w_qkv, w_out, w_up, w_down, slot_mol, slot_fill, cotangent
):
    rows_dev = tokens_in.shape[0]
    head_count = lax.axis_size("head")
    group_rows = rows_dev * head_count
    local_width = w_out.shape[0]
    local_heads = local_width // HEAD_DIM
    query_scale = HEAD_DIM ** (-0.5)
    block_rows = min(512, group_rows)
    block_count = group_rows // block_rows
    key_window = block_rows + 2 * SLOT_LEN
    padded_rows = group_rows + 2 * SLOT_LEN
    mol_rows = jnp.repeat(slot_mol[0], SLOT_LEN)
    fill_rows = jnp.repeat(slot_fill[0], SLOT_LEN)
    live_rows = jnp.arange(group_rows, dtype=jnp.int32) % SLOT_LEN < fill_rows
    mol_keys = jnp.pad(mol_rows, SLOT_LEN, constant_values=-1)
    live_keys = jnp.pad(live_rows, SLOT_LEN, constant_values=False)
    input_float = tokens_in.astype(jnp.float32)
    normed, norm_back = jax.vjp(layer_norm, input_float, gain_attn)
    normed_low = normed.astype(jnp.bfloat16)
    gathered = lax.all_gather(normed_low, "head", axis=0, tiled=True)
    column_scale = jnp.array([query_scale, 1.0, 1.0], jnp.float32)[:, None, None]
    projected = jnp.einsum("td,cde->cte", gathered, w_qkv, preferred_element_type=jnp.float32)
    projected_low = (projected * column_scale).astype(jnp.bfloat16)
    queries = projected_low[0].reshape(group_rows, local_heads, HEAD_DIM)
    pad_rows = ((SLOT_LEN, SLOT_LEN), (0, 0))
    keys_pad = jnp.pad(projected_low[1], pad_rows).reshape(padded_rows, local_heads, HEAD_DIM)
    values_pad = jnp.pad(projected_low[2], pad_rows).reshape(padded_rows, local_heads, HEAD_DIM)

    def scores_of(first_row):
        query_block = lax.dynamic_slice_in_dim(queries, first_row, block_rows, 0)
        key_block = lax.dynamic_slice_in_dim(keys_pad, first_row, key_window, 0)
        mol_block = lax.dynamic_slice_in_dim(mol_rows, first_row, block_rows, 0)
        mol_window = lax.dynamic_slice_in_dim(mol_keys, first_row, key_window, 0)
        live_window = lax.dynamic_slice_in_dim(live_keys, first_row, key_window, 0)
        allowed = (mol_block[:, None] == mol_window[None, :]) & live_window[None, :]
        raw_scores = jnp.einsum(
            "qhe,khe->hqk", query_block, key_block, preferred_element_type=jnp.float32
        )
        return jnp.where(allowed[None], raw_scores, masked_score)

    def attend(block_index):
        first_row = block_index * block_rows
        scores = scores_of(first_row)
        row_max = jnp.max(scores, axis=-1, keepdims=True)
        exp_scores = jnp.exp(scores - row_max)
        row_sum = jnp.sum(exp_scores, axis=-1, keepdims=True)
        probs_low = (exp_scores / row_sum).astype(jnp.bfloat16)
        value_block = lax.dynamic_slice_in_dim(values_pad, first_row, key_window, 0)
        mixed_block = jnp.einsum(
            "hqk,khe->qhe", probs_low, value_block, preferred_element_type=jnp.float32
        )
        return (
            mixed_block.reshape(block_rows, local_width).astype(jnp.bfloat16),
            (row_max + jnp.log(row_sum))[..., 0],
        )

    mixed_heads, log_sums = lax.map(attend, jnp.arange(block_count, dtype=jnp.int32))
    mixed_heads = mixed_heads.reshape(group_rows, local_width)
    mixed_rows = mixed_heads
    branch = lax.psum_scatter(
        jnp.dot(mixed_rows, w_out, preferred_element_type=jnp.float32),
        "head",
        scatter_dimension=0,
        tiled=True,
    )
    residual = input_float + branch
    normed_ffn, norm_ffn_back = jax.vjp(layer_norm, residual, gain_ffn)
    normed_ffn_low = normed_ffn.astype(jnp.bfloat16)
    ffn_inner = jnp.dot(normed_ffn_low, w_up, preferred_element_type=jnp.float32)
    activated, gelu_back = jax.vjp(gelu_exact, ffn_inner)
    hidden = activated.astype(jnp.bfloat16)
    output = (residual + jnp.dot(hidden, w_down, preferred_element_type=jnp.float32)).astype(
        jnp.bfloat16
    )
    grad_down = jnp.einsum("rf,rd->fd", hidden, cotangent, preferred_element_type=jnp.float32)
    d_hidden = jnp.einsum("rd,fd->rf", cotangent, w_down, preferred_element_type=jnp.float32)
    d_inner = gelu_back(d_hidden)[0].astype(jnp.bfloat16)
    grad_up = jnp.einsum("rd,rf->df", normed_ffn_low, d_inner, preferred_element_type=jnp.float32)
    d_normed_ffn = jnp.einsum("rf,df->rd", d_inner, w_up, preferred_element_type=jnp.float32)
    d_residual_norm, grad_gain_ffn = norm_ffn_back(d_normed_ffn)
    d_residual = cotangent.astype(jnp.float32) + d_residual_norm
    d_branch = d_residual.astype(jnp.bfloat16)
    shard_rows = lax.all_gather(d_branch, "head", axis=0, tiled=True)
    mixed_rows = mixed_heads
    grad_acc = jnp.einsum("te,td->ed", mixed_rows, shard_rows, preferred_element_type=jnp.float32)
    d_rows = jnp.einsum("td,ed->te", shard_rows, w_out, preferred_element_type=jnp.float32)
    grad_out = grad_acc
    d_mixed_low = d_rows.astype(jnp.bfloat16).reshape(group_rows, local_heads, HEAD_DIM)

    def back_block(running, block_index):
        d_key_acc, d_value_acc = running
        first_row = block_index * block_rows
        scores = scores_of(first_row)
        attn_probs = jnp.exp(scores - log_sums[block_index][:, :, None])
        probs_low = attn_probs.astype(jnp.bfloat16)
        query_block = lax.dynamic_slice_in_dim(queries, first_row, block_rows, 0)
        key_block = lax.dynamic_slice_in_dim(keys_pad, first_row, key_window, 0)
        value_block = lax.dynamic_slice_in_dim(values_pad, first_row, key_window, 0)
        grad_block = lax.dynamic_slice_in_dim(d_mixed_low, first_row, block_rows, 0)
        d_probs = jnp.einsum(
            "qhe,khe->hqk", grad_block, value_block, preferred_element_type=jnp.float32
        )
        inner_sum = jnp.sum(attn_probs * d_probs, axis=-1, keepdims=True)
        d_scores = (attn_probs * (d_probs - inner_sum)).astype(jnp.bfloat16)
        d_query = query_scale * jnp.einsum(
            "hqk,khe->qhe", d_scores, key_block, preferred_element_type=jnp.float32
        )
        d_key_block = jnp.einsum(
            "hqk,qhe->khe", d_scores, query_block, preferred_element_type=jnp.float32
        )
        d_value_block = jnp.einsum(
            "hqk,qhe->khe", probs_low, grad_block, preferred_element_type=jnp.float32
        )
        key_part = lax.dynamic_slice_in_dim(d_key_acc, first_row, key_window, 0)
        d_key_acc = lax.dynamic_update_slice_in_dim(d_key_acc, key_part + d_key_block, first_row, 0)
        value_part = lax.dynamic_slice_in_dim(d_value_acc, first_row, key_window, 0)
        d_value_acc = lax.dynamic_update_slice_in_dim(
            d_value_acc, value_part + d_value_block, first_row, 0
        )
        return ((d_key_acc, d_value_acc), d_query.astype(jnp.bfloat16))

    zero_pad = jnp.zeros((padded_rows, local_heads, HEAD_DIM), jnp.float32)
    (d_key_acc, d_value_acc), d_query = lax.scan(
        back_block, (zero_pad, zero_pad), jnp.arange(block_count, dtype=jnp.int32)
    )
    d_query = d_query.reshape(group_rows, local_width)
    d_key = (
        d_key_acc[SLOT_LEN : SLOT_LEN + group_rows]
        .reshape(group_rows, local_width)
        .astype(jnp.bfloat16)
    )
    d_value = (
        d_value_acc[SLOT_LEN : SLOT_LEN + group_rows]
        .reshape(group_rows, local_width)
        .astype(jnp.bfloat16)
    )
    d_qkv = jnp.stack([d_query, d_key, d_value])
    grad_qkv = jnp.einsum("td,cte->cde", gathered, d_qkv, preferred_element_type=jnp.float32)
    d_normed = lax.psum_scatter(
        jnp.einsum("cte,cde->td", d_qkv, w_qkv, preferred_element_type=jnp.float32).astype(
            jnp.bfloat16
        ),
        "head",
        scatter_dimension=0,
        tiled=True,
    ).astype(jnp.float32)
    d_input_norm, grad_gain_attn = norm_back(d_normed)
    d_tokens = d_residual + d_input_norm
    grad_qkv, grad_out = lax.psum((grad_qkv, grad_out), "dp")
    grad_up, grad_down, grad_gain_attn, grad_gain_ffn = lax.psum(
        (grad_up, grad_down, grad_gain_attn, grad_gain_ffn), ("dp", "head")
    )
    return (output, d_tokens, grad_gain_attn, grad_gain_ffn, grad_qkv, grad_out, grad_up, grad_down)


def solution(mesh):
    return jax.shard_map(
        local,
        mesh=mesh,
        in_specs=(
            P(("dp", "head"), None),
            P(),
            P(),
            P(None, None, "head"),
            P("head", None),
            P(),
            P(),
            P("dp", None),
            P("dp", None),
            P(("dp", "head"), None),
        ),
        out_specs=(
            P(("dp", "head"), None),
            P(("dp", "head"), None),
            P(),
            P(),
            P(None, None, "head"),
            P("head", None),
            P(),
            P(),
        ),
        check_vma=False,
    )
```

profile of v0, /device:TPU:0, one launch (start us, length us, event | category | flops | bytes accessed | tf_op | source)
XLA Modules:
  0.0 744.3 jit_solution(16228574355169517621)
XLA Ops:
  13.0 66.1 %all-gather.3.cloned.1.call-done = bf16[2048,768]{1,0:T(8,128)(2,1)} async-done(((bf16[512,768]{1,0:T(8,128)(2,1)}), bf16[2048,768]{1,0:T(8,128)(2,1)}) %all-gather.3.cloned.1.call-update) | async-done | bytes 3145744 | tf_op jit(solution)/shard_map/all_gather | solution.py:44
  79.0 3.9 fusion.80
  85.8 52.1 %while.26 = (s32[]{:T(128)}, bf16[4,512,192]{1,2,0:T(8,128)(2,1)}, f32[4,8,512]{2,1,0:T(8,128)S(1)}, s32[4]{0:T(128)S(1)}, bf16[2304,8,24]{0,2,1:T(8,128)(2,1)},...) while((s32[]{:T(128)}, bf16[4,512,192]{1,2,0:T(8,128)(2,1)}, ...), condition=%wide.region_5.6_spmd, body=%wide.region_2.5_spmd.sunk | while | flops 331182080 | bytes 40846856 | solution.py:81
  93.6 4.5 fusion.122
  106.6 4.5 fusion.122
  119.6 4.5 fusion.122
  132.7 4.5 fusion.122
  140.0 3.7 fusion.81
  143.9 109.4 %reduce-scatter.3.cloned.1.call-done = f32[512,768]{1,0:T(8,128)} async-done(((f32[2048,768]{1,0:T(8,128)}), f32[512,768]{1,0:T(8,128)}) %reduce-scatter.3.cloned.1.call-update) | async-done | bytes 1572880 | tf_op jit(solution)/shard_map/reduce_scatter | solution.py:84
  257.9 5.1 add_convert_fusion
  267.7 64.0 %all-gather.5.cloned.1.call-done = bf16[2048,768]{1,0:T(8,128)(2,1)} async-done(((bf16[512,768]{1,0:T(8,128)(2,1)}), bf16[2048,768]{1,0:T(8,128)(2,1)}) %all-gather.5.cloned.1.call-update) | async-done | bytes 3145744 | tf_op jit(solution)/shard_map/all_gather | solution.py:107
  337.4 104.5 %while.27 = (s32[]{:T(128)}, f32[2304,8,24]{0,2,1:T(8,128)}, f32[2304,8,24]{0,2,1:T(8,128)}, bf16[4,512,8,24]{1,3,2,0:T(8,128)(2,1)}, s32[4]{0:T(128)S(1)}, /*in...) while((s32[]{:T(128)}, f32[2304,8,24]{0,2,1:T(8,128)}, ...), condition=%wide.region_13.14_spmd, body=%wide.region_11.13_spmd.sunk | while | flops 793997312 | bytes 113673928 | solution.py:147
  344.1 4.5 fusion.133
  348.5 5.3 multiply_reduce_fusion.5
  357.1 3.4 fusion.134
  370.2 4.5 fusion.133
  374.7 5.3 multiply_reduce_fusion.5
  383.2 3.4 fusion.134
  396.3 4.5 fusion.133
  400.8 5.3 multiply_reduce_fusion.5
  409.3 3.4 fusion.134
  422.4 4.5 fusion.133
  426.9 5.3 multiply_reduce_fusion.5
  432.2 3.2 multiply_convert_fusion.7
  435.5 3.4 fusion.134
  448.8 4.1 bitcast_convert_fusion
  465.7 5.1 fusion.62
  470.8 41.3 %reduce-scatter.5.cloned.1.call-done = bf16[512,768]{1,0:T(8,128)(2,1)} async-done(((bf16[2048,768]{1,0:T(8,128)(2,1)}), bf16[512,768]{1,0:T(8,128)(2,1)}) %reduce-scatter.5.cloned.1.call-update) | async-done | bytes 786448 | tf_op jit(solution)/shard_map/reduce_scatter | solution.py:163
  517.1 40.9 %all-reduce.4 = (f32[768]{0:T(1024)}, f32[768]{0:T(1024)}) all-reduce(f32[768]{0:T(1024)} %get-tuple-element.137, f32[768]{0:T(1024)} %get-tuple-element.135), channel_id=1, replica_groups=mesh['dp'=8,'head'=4] {'dp','head'}, use_global_device_ids=true, to_apply=%region_18.19 | all-reduce | flops 1536 | bytes 12288 | tf_op jit(solution)/shard_map/psum | solution.py:174
  558.7 3.4 add_add_fusion.2
  562.1 102.0 %all-reduce.10.cloned.1.call-done = (f32[768,768]{1,0:T(8,128)}, f32[768,768]{1,0:T(8,128)}) async-done(((f32[768,768]{1,0:T(8,128)}, f32[768,768]{1,0:T(8,128)}), (f32[768,768]{1,0:T(8,128)}, f32[768,768]{1,0:T(8,128)})) %all-reduce.10.cloned.1.call-update) | async-done | bytes 4718608 | tf_op jit(solution)/shard_map/psum | solution.py:174
  664.1 65.6 %all-reduce.12.cloned.1.call-done = (f32[3,768,192]{1,2,0:T(8,128)}, f32[192,768]{1,0:T(8,128)}) async-done(((f32[3,768,192]{1,2,0:T(8,128)}, f32[192,768]{1,0:T(8,128)}), (f32[3,768,192]{1,2,0:T(8,128)}, f32[192,768]{1,0:T(8,128)})) %all-reduce.12.cloned.1.call-update) | async-done | bytes 2359312 | tf_op jit(solution)/shard_map/psum | solution.py:173
  (258 shorter events, 128.2 us)
Async XLA Ops:
  7.2 250.5 %copy-start = (bf16[768,768]{1,0:T(8,128)(2,1)S(1)}, bf16[768,768]{1,0:T(8,128)(2,1)}, u32[]{:S(2)}) copy-start(bf16[768,768]{1,0:T(8,128)(2,1)} %param.21) | copy-start | bytes 3538948
  7.2 4.3 copy-start.1
  7.2 4.3 copy-start.33
  7.2 71.8 %all-gather.3.cloned.1.call-start = ((), (), s32[]{:S(2)}) async-start(), calls=%async_computation.2 | async-start | bytes 3932160 | tf_op jit(solution)/shard_map/all_gather | solution.py:44
  8.7 4.1 copy-start.46
  8.7 4.2 copy-start.47
  8.7 70.3 %copy-start.49 = (bf16[3,768,192]{1,2,0:T(8,128)(2,1)S(1)}, bf16[3,768,192]{1,2,0:T(8,128)(2,1)}, u32[]{:S(2)}) copy-start(bf16[3,768,192]{1,2,0:T(8,128)(2,1)} %param.18) | copy-start | bytes 2654212
  12.7 240.6 %reduce-scatter.3.cloned.1.call-start = ((), (), s32[]{:S(2)}) async-start(), calls=%async_computation.3 | async-start | bytes 7864320 | tf_op jit(solution)/shard_map/reduce_scatter | solution.py:84
  79.0 3.9 copy-start.45
  143.7 188.0 %all-gather.5.cloned.1.call-start = ((), (), s32[]{:S(2)}) async-start(), calls=%async_computation.4 | async-start | bytes 3932160 | tf_op jit(solution)/shard_map/all_gather | solution.py:107
  254.9 9.7 %copy-start.5 = (f32[512,768]{1,0:T(8,128)}, f32[512,768]{1,0:T(8,128)S(1)}, u32[]{:S(2)}) copy-start(f32[512,768]{1,0:T(8,128)S(1)} %get-tuple-element.196) | copy-start | bytes 4718596
  255.0 9.6 %copy-start.37 = (f32[512]{0:T(512)}, f32[512]{0:T(512)S(1)}, u32[]{:S(2)}) copy-start(f32[512]{0:T(512)S(1)} %broadcast_multiply_fusion) | copy-start | bytes 6148
  256.8 7.8 %copy-start.39 = (f32[512]{0:T(512)}, f32[512]{0:T(512)S(1)}, u32[]{:S(2)}) copy-start(f32[512]{0:T(512)S(1)} %fusion.72) | copy-start | bytes 6148
  257.9 5.1 copy-start.19
  267.6 244.6 %reduce-scatter.5.cloned.1.call-start = ((), (), s32[]{:S(2)}) async-start(), calls=%async_computation.5 | async-start | bytes 3932160 | tf_op jit(solution)/shard_map/reduce_scatter | solution.py:163
  337.4 6.6 copy-start.3
  337.4 6.6 copy-start.14
  363.6 6.6 copy-start.3
  363.6 6.6 copy-start.14
  389.7 6.6 copy-start.3
  389.7 6.6 copy-start.14
  415.8 6.6 copy-start.3
  415.8 6.6 copy-start.14
  444.3 4.6 copy-start.50
  453.0 211.2 %all-reduce.10.cloned.1.call-start = ((), (), s32[]{:S(2)}) async-start(), calls=%async_computation.6 | async-start | bytes 9437184 | tf_op jit(solution)/shard_map/psum | solution.py:174
  461.0 268.8 %all-reduce.12.cloned.1.call-start = ((), (), s32[]{:S(2)}) async-start(), calls=%async_computation.7 | async-start | bytes 4718592 | tf_op jit(solution)/shard_map/psum | solution.py:173
  470.8 41.4 %copy-start.2 = (bf16[512,768]{1,0:T(8,128)(2,1)S(1)}, bf16[512,768]{1,0:T(8,128)(2,1)}, u32[]{:S(2)}) copy-start(bf16[512,768]{1,0:T(8,128)(2,1)} %param.15) | copy-start | bytes 2359300
  470.8 41.4 %copy-start.32 = (f32[512]{0:T(512)S(1)}, f32[512]{0:T(512)}, u32[]{:S(2)}) copy-start(f32[512]{0:T(512)} %copy-done.31) | copy-start | bytes 6148
  470.8 41.4 %copy-start.34 = (f32[768]{0:T(1024)S(1)}, f32[768]{0:T(1024)}, u32[]{:S(2)}) copy-start(f32[768]{0:T(1024)} %param.16) | copy-start | bytes 9220
  470.8 43.7 %copy-start.36 = (f32[512]{0:T(512)S(1)}, f32[512]{0:T(512)}, u32[]{:S(2)}) copy-start(f32[512]{0:T(512)} %copy-done.35) | copy-start | bytes 6148
  470.8 87.9 %copy-start.8 = (f32[512,768]{1,0:T(8,128)S(1)}, f32[512,768]{1,0:T(8,128)}, u32[]{:S(2)}) copy-start(f32[512,768]{1,0:T(8,128)} %copy-done.7) | copy-start | bytes 4718596
  729.8 3.8 copy-start.18
  (37 other events, 79.3 us)
Sparse Core Ops, SparseCore 0:
  12.8 66.1 all-gather.2
  143.8 109.4 reduce-scatter.2
  267.7 63.9 all-gather.4
  453.1 59.0 reduce-scatter.4
  518.4 145.6 all-reduce.9
  667.9 61.8 all-reduce.11
where the time goes:
time: 746 us; the launch traced here: 744 us
  waiting for transfers between devices  449 us (60%)
  matrix products  143 us (19%)
  other arithmetic  46.8 us (6%)
  blocking collectives  40.9 us (5%)
  local copies, waits for them, and re-layouts  37.4 us (5%)
  between operations  14.6 us (2%)
  loops' own time  13.1 us (2%)
    reduce_scatter x1, waiting for transfers between devices, local(): lax.psum_scatter(jnp.dot(mixed_rows, w_out, preferred_element_type=jnp.fl...  109 us
    psum x1, waiting for transfers between devices, local(): lax.psum((grad_up, grad_down, grad_gain_attn, grad_gain_ffn), ('dp', 'hea...  102 us
    all_gather x1, waiting for transfers between devices, local(): gathered = lax.all_gather(normed_low, 'head', axis=0, tiled=True)  66.1 us
    psum x1, waiting for transfers between devices, local(): grad_qkv, grad_out = lax.psum((grad_qkv, grad_out), 'dp')  65.6 us
    all_gather x1, waiting for transfers between devices, local(): shard_rows = lax.all_gather(d_branch, 'head', axis=0, tiled=True)  64 us
    reduce_scatter x1, waiting for transfers between devices, local(): lax.psum_scatter(jnp.einsum('cte,cde->td', d_qkv, w_qkv, preferred_elemen...  41.3 us
    psum x1, blocking collectives, local(): lax.psum((grad_up, grad_down, grad_gain_attn, grad_gain_ffn), ('dp', 'hea...  40.9 us
    dot_general x8, matrix products, scores_of(): jnp.einsum('qhe,khe->hqk', query_block, key_block, preferred_element_type...  23.2 us
  transfers between devices with their start and end apart: 6, of which 6 were waited for; matrix products, arithmetic and copies ran while one was open for 3% of the time, Pallas kernels for 0%

commit v1 on v0

--- a/solution.py
+++ b/solution.py
@@ -7,6 +7,23 @@
 SLOT_LEN = 128
 epsilon = 1e-05
 masked_score = -1000000000.0
+
+
+def joined_along(tiles, dim):
+    tiles = jnp.moveaxis(tiles, 0, dim)
+    lengths = tiles.shape
+    return tiles.reshape(*lengths[:dim], lengths[dim] * lengths[dim + 1], *lengths[dim + 2 :])
+
+
+def doubled(value, axis):
+    count, index = (lax.axis_size(axis), lax.axis_index(axis))
+    blocks, bit = (value[None], 1)
+    while bit < count:
+        other = lax.ppermute(blocks, axis, [(i, i ^ bit) for i in range(count)])
+        low = index & bit == 0
+        blocks = jnp.concatenate([jnp.where(low, blocks, other), jnp.where(low, other, blocks)])
+        bit *= 2
+    return blocks
 
 
 def layer_norm(values, scale_gain):
@@ -41,7 +58,7 @@
     input_float = tokens_in.astype(jnp.float32)
     normed, norm_back = jax.vjp(layer_norm, input_float, gain_attn)
     normed_low = normed.astype(jnp.bfloat16)
-    gathered = lax.all_gather(normed_low, "head", axis=0, tiled=True)
+    gathered = joined_along(doubled(normed_low, "head"), 0)
     column_scale = jnp.array([query_scale, 1.0, 1.0], jnp.float32)[:, None, None]
     projected = jnp.einsum("td,cde->cte", gathered, w_qkv, preferred_element_type=jnp.float32)
     projected_low = (projected * column_scale).astype(jnp.bfloat16)

time: 746 us -> 783 us (1.050)
  starting transfers between devices: 0.43 us -> 17.4 us
  waiting for transfers between devices: 449 us -> 458 us
    ppermute x0 -> x2, waiting for transfers between devices: none -> 84.6 us  [doubled(): other = lax.ppermute(blocks, axis, [(i, i ^ bit) for i in range(count)])]
    all_gather x1 -> x0, waiting for transfers between devices: 66.1 us -> none  [local(): gathered = lax.all_gather(normed_low, 'head', axis=0, tiled=True)]
    all_gather x1, starting transfers between devices: 0.22 us -> 11.4 us  [local(): shard_rows = lax.all_gather(d_branch, 'head', axis=0, tiled=True)]
    reduce_scatter x1, waiting for transfers between devices: 109 us -> 101 us  [local(): lax.psum_scatter(jnp.dot(mixed_rows, w_out, preferred_element_type=jnp.fl...]
    unnamed x98 -> x106, local copies, waits for them, and re-layouts: 15.4 us -> 16.8 us
  transfers between devices with their start and end apart: 6 -> 7, of which waited for: 6 -> 7; matrix products, arithmetic and copies ran while one was open for 3% -> 3% of each run, Pallas kernels for 0% -> 0%
where the time goes in v1:
time: 783 us; the launch traced here: 774 us
  waiting for transfers between devices  458 us (58%)
  matrix products  140 us (18%)
  other arithmetic  50.6 us (6%)
  blocking collectives  40.9 us (5%)
  local copies, waits for them, and re-layouts  39 us (5%)
  starting transfers between devices  17.4 us (2%)
  between operations  14.7 us (2%)
  loops' own time  12.9 us (2%)
    psum x1, waiting for transfers between devices, local(): lax.psum((grad_up, grad_down, grad_gain_attn, grad_gain_ffn), ('dp', 'hea...  102 us
    reduce_scatter x1, waiting for transfers between devices, local(): lax.psum_scatter(jnp.dot(mixed_rows, w_out, preferred_element_type=jnp.fl...  101 us
    ppermute x2, waiting for transfers between devices, doubled(): other = lax.ppermute(blocks, axis, [(i, i ^ bit) for i in range(count)])  84.6 us
    psum x1, waiting for transfers between devices, local(): grad_qkv, grad_out = lax.psum((grad_qkv, grad_out), 'dp')  65.6 us
    all_gather x1, waiting for transfers between devices, local(): shard_rows = lax.all_gather(d_branch, 'head', axis=0, tiled=True)  64.1 us
    reduce_scatter x1, waiting for transfers between devices, local(): lax.psum_scatter(jnp.einsum('cte,cde->td', d_qkv, w_qkv, preferred_elemen...  41.5 us
    psum x1, blocking collectives, local(): lax.psum((grad_up, grad_down, grad_gain_attn, grad_gain_ffn), ('dp', 'hea...  40.9 us
    dot_general x8, matrix products, scores_of(): jnp.einsum('qhe,khe->hqk', query_block, key_block, preferred_element_type...  23.2 us
  transfers between devices with their start and end apart: 7, of which 7 were waited for; matrix products, arithmetic and copies ran while one was open for 3% of the time, Pallas kernels for 0%

profile of v1, /device:TPU:0, one launch (start us, length us, event | category | flops | bytes accessed | tf_op | source)
XLA Modules:
  0.0 773.8 jit_solution(8368778512674738803)
XLA Ops:
  14.2 17.6 %collective-permute-done = bf16[1,512,768]{2,1,0:T(8,128)(2,1)} collective-permute-done((bf16[1,512,768]{2,1,0:T(8,128)(2,1)S(1)}, bf16[1,512,768]{2,1,0:T(8,128)(2,1)}, u32[]{:S(2)}, u32[]{:S(2)}) %collective-permute-start) | collective-permute-done | bytes 786464 | tf_op jit(solution)/shard_map/ppermute | solution.py:22
  38.4 67.0 %collective-permute-done.1 = bf16[2,512,768]{2,1,0:T(8,128)(2,1)} collective-permute-done((bf16[2,512,768]{2,1,0:T(8,128)(2,1)}, bf16[2,512,768]{2,1,0:T(8,128)(2,1)}, u32[]{:S(2)}, u32[]{:S(2)}) %collective-permute-start.1) | collective-permute-done | bytes 1572896 | tf_op jit(solution)/shard_map/ppermute | solution.py:22
  112.9 52.1 %while.26 = (s32[]{:T(128)}, bf16[4,512,192]{1,2,0:T(8,128)(2,1)}, f32[4,8,512]{2,1,0:T(8,128)S(1)}, s32[4]{0:T(128)S(1)}, bf16[2304,8,24]{0,2,1:T(8,128)(2,1)},...) while((s32[]{:T(128)}, bf16[4,512,192]{1,2,0:T(8,128)(2,1)}, ...), condition=%wide.region_5.6_spmd, body=%wide.region_2.5_spmd.sunk | while | flops 331182080 | bytes 40846856 | solution.py:98
  120.8 4.5 fusion.119
  133.8 4.5 fusion.119
  146.8 4.5 fusion.119
  159.8 4.5 fusion.119
  167.2 3.7 fusion.77
  170.9 11.4 %all-gather.2.cloned.1.call-start = ((), (), s32[]{:S(2)}) async-start(), calls=%async_computation.3 | async-start | bytes 3932160 | tf_op jit(solution)/shard_map/all_gather | solution.py:124
  182.3 100.5 %reduce-scatter.3.cloned.1.call-done = f32[512,768]{1,0:T(8,128)} async-done(((f32[2048,768]{1,0:T(8,128)}), f32[512,768]{1,0:T(8,128)}) %reduce-scatter.3.cloned.1.call-update) | async-done | bytes 1572880 | tf_op jit(solution)/shard_map/reduce_scatter | solution.py:101
  287.4 5.1 add_convert_fusion
  297.2 64.1 %all-gather.2.cloned.1.call-done = bf16[2048,768]{1,0:T(8,128)(2,1)} async-done(((bf16[512,768]{1,0:T(8,128)(2,1)}), bf16[2048,768]{1,0:T(8,128)(2,1)}) %all-gather.2.cloned.1.call-update) | async-done | bytes 3145744 | tf_op jit(solution)/shard_map/all_gather | solution.py:124
  367.0 104.5 %while.27 = (s32[]{:T(128)}, f32[2304,8,24]{0,2,1:T(8,128)}, f32[2304,8,24]{0,2,1:T(8,128)}, bf16[4,512,8,24]{1,3,2,0:T(8,128)(2,1)}, s32[4]{0:T(128)S(1)}, /*in...) while((s32[]{:T(128)}, f32[2304,8,24]{0,2,1:T(8,128)}, ...), condition=%wide.region_13.14_spmd, body=%wide.region_11.13_spmd.sunk | while | flops 793997312 | bytes 113673928 | solution.py:164
  373.6 4.5 fusion.130
  378.1 5.3 multiply_reduce_fusion.5
  386.6 3.4 fusion.131
  399.7 4.5 fusion.130
  404.2 5.3 multiply_reduce_fusion.5
  412.7 3.4 fusion.131
  425.9 4.5 fusion.130
  430.3 5.3 multiply_reduce_fusion.5
  438.9 3.4 fusion.131
  452.0 4.5 fusion.130
  456.5 5.3 multiply_reduce_fusion.5
  465.0 3.4 fusion.131
  478.3 4.1 bitcast_convert_fusion
  495.8 4.4 convolution_bitcast_fusion.1
  500.2 41.5 %reduce-scatter.5.cloned.1.call-done = bf16[512,768]{1,0:T(8,128)(2,1)} async-done(((bf16[2048,768]{1,0:T(8,128)(2,1)}), bf16[512,768]{1,0:T(8,128)(2,1)}) %reduce-scatter.5.cloned.1.call-update) | async-done | bytes 786448 | tf_op jit(solution)/shard_map/reduce_scatter | solution.py:180
  546.7 40.9 %all-reduce.4 = (f32[768]{0:T(1024)}, f32[768]{0:T(1024)}) all-reduce(f32[768]{0:T(1024)} %get-tuple-element.137, f32[768]{0:T(1024)} %get-tuple-element.135), channel_id=1, replica_groups=mesh['dp'=8,'head'=4] {'dp','head'}, use_global_device_ids=true, to_apply=%region_18.19 | all-reduce | flops 1536 | bytes 12288 | tf_op jit(solution)/shard_map/psum | solution.py:191
  588.3 3.4 add_add_fusion.2
  591.6 102.0 %all-reduce.10.cloned.1.call-done = (f32[768,768]{1,0:T(8,128)}, f32[768,768]{1,0:T(8,128)}) async-done(((f32[768,768]{1,0:T(8,128)}, f32[768,768]{1,0:T(8,128)}), (f32[768,768]{1,0:T(8,128)}, f32[768,768]{1,0:T(8,128)})) %all-reduce.10.cloned.1.call-update) | async-done | bytes 4718608 | tf_op jit(solution)/shard_map/psum | solution.py:191
  693.7 65.6 %all-reduce.12.cloned.1.call-done = (f32[3,768,192]{1,2,0:T(8,128)}, f32[192,768]{1,0:T(8,128)}) async-done(((f32[3,768,192]{1,2,0:T(8,128)}, f32[192,768]{1,0:T(8,128)}), (f32[3,768,192]{1,2,0:T(8,128)}, f32[192,768]{1,0:T(8,128)})) %all-reduce.12.cloned.1.call-update) | async-done | bytes 2359312 | tf_op jit(solution)/shard_map/psum | solution.py:190
  (271 shorter events, 144.4 us)
Async XLA Ops:
  7.2 280.0 %copy-start = (bf16[768,768]{1,0:T(8,128)(2,1)S(1)}, bf16[768,768]{1,0:T(8,128)(2,1)}, u32[]{:S(2)}) copy-start(bf16[768,768]{1,0:T(8,128)(2,1)} %param.21) | copy-start | bytes 3538948
  7.2 275.6 %reduce-scatter.3.cloned.1.call-start = ((), (), s32[]{:S(2)}) async-start(), calls=%async_computation.2 | async-start | bytes 7864320 | tf_op jit(solution)/shard_map/reduce_scatter | solution.py:101
  8.7 24.8 %copy-start.37 = (f32[512]{0:T(512)}, f32[512]{0:T(512)S(1)}, u32[]{:S(2)}) copy-start(f32[512]{0:T(512)S(1)} %broadcast_multiply_fusion.1) | copy-start | bytes 6148
  10.8 22.7 %copy-start.39 = (f32[512]{0:T(512)}, f32[512]{0:T(512)S(1)}, u32[]{:S(2)}) copy-start(f32[512]{0:T(512)S(1)} %fusion.67) | copy-start | bytes 6148
  11.1 20.8 %collective-permute-start = (bf16[1,512,768]{2,1,0:T(8,128)(2,1)S(1)}, bf16[1,512,768]{2,1,0:T(8,128)(2,1)}, u32[]{:S(2)}, u32[]{:S(2)}) collective-permute-start(bf16[1,512,768]{2,1,0:T(8,128)(2,1)S(1)} %fusion.62), channel_id=1, source_target_pairs={{0,1},{1,0},{2,3},{3,2},{4,5},{5,4},{6,7},{7,6},{8,9},{9,8},{10,11... | collective-permute-start | bytes 2359304 | tf_op jit(solution)/shard_map/ppermute | solution.py:22
  33.5 4.1 copy-start.50
  33.6 4.1 copy-start.51
  34.9 70.5 %collective-permute-start.1 = (bf16[2,512,768]{2,1,0:T(8,128)(2,1)}, bf16[2,512,768]{2,1,0:T(8,128)(2,1)}, u32[]{:S(2)}, u32[]{:S(2)}) collective-permute-start(bf16[2,512,768]{2,1,0:T(8,128)(2,1)} %pad_maximum_fusion.2), channel_id=1, source_target_pairs={{0,2},{1,3},{2,0},{3,1},{4,6},{5,7},{6,4},{7,5},{8,10},{9,11},{10,... | collective-permute-start | bytes 4718600 | tf_op jit(solution)/shard_map/ppermute | solution.py:22
  170.9 190.4 %all-gather.2.cloned.1.call-start = ((), (), s32[]{:S(2)}) async-start(), calls=%async_computation.3 | async-start | bytes 3932160 | tf_op jit(solution)/shard_map/all_gather | solution.py:124
  284.4 9.7 %copy-start.5 = (f32[512,768]{1,0:T(8,128)}, f32[512,768]{1,0:T(8,128)S(1)}, u32[]{:S(2)}) copy-start(f32[512,768]{1,0:T(8,128)S(1)} %get-tuple-element.196) | copy-start | bytes 4718596
  284.5 9.6 %copy-start.41 = (f32[512]{0:T(512)}, f32[512]{0:T(512)S(1)}, u32[]{:S(2)}) copy-start(f32[512]{0:T(512)S(1)} %broadcast_multiply_fusion) | copy-start | bytes 6148
  286.3 7.8 %copy-start.43 = (f32[512]{0:T(512)}, f32[512]{0:T(512)S(1)}, u32[]{:S(2)}) copy-start(f32[512]{0:T(512)S(1)} %fusion.68) | copy-start | bytes 6148
  287.4 5.1 copy-start.21
  297.1 244.6 %reduce-scatter.5.cloned.1.call-start = ((), (), s32[]{:S(2)}) async-start(), calls=%async_computation.4 | async-start | bytes 3932160 | tf_op jit(solution)/shard_map/reduce_scatter | solution.py:180
  367.0 6.6 copy-start.3
  367.0 6.6 copy-start.14
  393.1 6.6 copy-start.3
  393.1 6.6 copy-start.14
  419.2 6.6 copy-start.3
  419.2 6.6 copy-start.14
  445.4 6.6 copy-start.3
  445.4 6.6 copy-start.14
  473.8 4.5 copy-start.54
  482.5 211.2 %all-reduce.10.cloned.1.call-start = ((), (), s32[]{:S(2)}) async-start(), calls=%async_computation.5 | async-start | bytes 9437184 | tf_op jit(solution)/shard_map/psum | solution.py:191
  490.5 268.8 %all-reduce.12.cloned.1.call-start = ((), (), s32[]{:S(2)}) async-start(), calls=%async_computation.6 | async-start | bytes 4718592 | tf_op jit(solution)/shard_map/psum | solution.py:190
  490.5 4.6 copy-start.28
  500.2 41.5 %copy-start.2 = (bf16[512,768]{1,0:T(8,128)(2,1)S(1)}, bf16[512,768]{1,0:T(8,128)(2,1)}, u32[]{:S(2)}) copy-start(bf16[512,768]{1,0:T(8,128)(2,1)} %param.15) | copy-start | bytes 2359300
  500.2 41.5 %copy-start.36 = (f32[768]{0:T(1024)S(1)}, f32[768]{0:T(1024)}, u32[]{:S(2)}) copy-start(f32[768]{0:T(1024)} %param.16) | copy-start | bytes 9220
  500.2 41.5 %copy-start.38 = (f32[512]{0:T(512)S(1)}, f32[512]{0:T(512)}, u32[]{:S(2)}) copy-start(f32[512]{0:T(512)} %copy-done.37) | copy-start | bytes 6148
  500.2 43.8 %copy-start.40 = (f32[512]{0:T(512)S(1)}, f32[512]{0:T(512)}, u32[]{:S(2)}) copy-start(f32[512]{0:T(512)} %copy-done.39) | copy-start | bytes 6148
  500.2 88.0 %copy-start.8 = (f32[512,768]{1,0:T(8,128)S(1)}, f32[512,768]{1,0:T(8,128)}, u32[]{:S(2)}) copy-start(f32[512,768]{1,0:T(8,128)} %copy-done.7) | copy-start | bytes 4718596
  759.2 3.8 copy-start.20
  (42 other events, 93.0 us)
Sparse Core Ops, SparseCore 0:
  171.0 111.7 reduce-scatter.2
  297.2 63.9 all-gather.1
  482.6 59.0 reduce-scatter.4
  547.9 145.6 all-reduce.9
  697.4 61.7 all-reduce.11
